TPU v7x, 32 devices: a whole 2x2x4 slice. The times are simulated.
32 devices in a mesh: context: 2 (over core), fheads: 4 (over y, x), seqs: 4 (over z).
Axes of the slice: x: 2, y: 2, z: 4, core: 2. Of those that a mesh axis runs over, the one named last changes fastest.
Arguments:
- query_rows: bfloat16 [4096, 3072], P(('seqs', 'context'), 'fheads'), parts along dimension 0, may hold values from -5 to 5
- key_rows: bfloat16 [4096, 3072], P(('seqs', 'context'), 'fheads'), parts along dimension 0, may hold values from -5 to 5
- value_rows: bfloat16 [4096, 3072], P(('seqs', 'context'), 'fheads'), parts along dimension 0, may hold values from -10 to 10
- step_sizes: float32 [4096, 4], P(('seqs', 'context'), 'fheads'), parts along dimension 0, may hold values from 2e-05 to 0.0018
- w_gate: bfloat16 [4, 768, 768], P('fheads', 'context'), may hold values from -4 to 4
- w_up: bfloat16 [4, 768, 768], P('fheads', 'context'), may hold values from -4 to 4
- w_down: bfloat16 [4, 768, 768], P('fheads', 'context'), may hold values from -4 to 4
Outputs:
- window_out: bfloat16 [4096, 3072], P(('seqs', 'context'), 'fheads'), parts along dimension 0
- fast_out: bfloat16 [4096, 3072], P(('seqs', 'context'), 'fheads'), parts along dimension 0
There are 4 independent parts, one for each index of `seqs`. A program takes and returns all parts, laid end to end along the dimension named above; an argument that names none is the same for every part. Nothing has to cross between parts.
All inputs are finite; a program needn't handle non-finite values.
Results may differ from a plain program's by a relative error of at most 0.035.
Values may be sent and summed in bfloat16 or wider, within the bound.
No kernel may reach another device: no remote copies, remote signals or barrier semaphores. Data moves between devices by JAX's collectives and lax.ppermute only.
A program may use at most 128 MiB of HBM per device.

v0:
```python
import math
import jax
import jax.numpy as jnp
from jax import lax
from jax.sharding import PartitionSpec as P

HD = 128
WINDOW = 512


def passed_along(x, axis, by):
    peers = lax.axis_size(axis)
    pairs = [(i, i + by) for i in range(peers) if 0 <= i + by < peers]
    return lax.ppermute(x, axis, pairs)


def unit_rows(values):
    return values * lax.rsqrt(jnp.mean(values * values, axis=-1, keepdims=True) + 1e-06)


def window_block(queries, keys_near, values_near, first_pos):
    row_count = queries.shape[0]
    query_pos = first_pos + jnp.arange(row_count, dtype=jnp.int32)
    key_pos = first_pos - WINDOW + jnp.arange(row_count + WINDOW, dtype=jnp.int32)
    allowed = (
        (key_pos[None, :] >= 0)
        & (key_pos[None, :] <= query_pos[:, None])
        & (key_pos[None, :] > query_pos[:, None] - WINDOW)
    )
    scores = jnp.einsum(
        "ihd,jhd->hij", queries, keys_near, preferred_element_type=jnp.float32
    ) / math.sqrt(HD)
    scores = jnp.where(allowed[None], scores, -1e30)
    row_max = jnp.max(scores, axis=-1, keepdims=True)
    powers = jnp.exp(scores - row_max)
    weights = (powers / jnp.sum(powers, axis=-1, keepdims=True)).astype(jnp.bfloat16)
    attended = jnp.einsum("hij,jhd->ihd", weights, values_near, preferred_element_type=jnp.float32)
    return attended.astype(jnp.bfloat16)


def dot_rows(first_op, second_op):
    return lax.dot_general(
        first_op, second_op, (((0,), (0,)), ((), ())), preferred_element_type=jnp.float32
    )


def dot_back(first_op, second_op):
    return lax.dot_general(
        first_op, second_op, (((1,), (1,)), ((), ())), preferred_element_type=jnp.float32
    )


def renormed(weight, gradient):
    initial = weight.astype(jnp.float32)
    fresh_rows = initial - gradient
    old_ms = jnp.mean(initial * initial, axis=0)
    new_ms = jnp.mean(fresh_rows * fresh_rows, axis=0)
    return (fresh_rows * jnp.sqrt(old_ms) * lax.rsqrt(new_ms + 1e-06)).astype(jnp.bfloat16)


def apply_fast(fast_queries, gate_w, up_w, down_w):
    gate_new = jnp.dot(fast_queries, gate_w, preferred_element_type=jnp.float32)
    up_new = jnp.dot(fast_queries, up_w, preferred_element_type=jnp.float32)
    hidden_new = (gate_new * jax.nn.sigmoid(gate_new) * up_new).astype(jnp.bfloat16)
    return jnp.dot(hidden_new, down_w, preferred_element_type=jnp.float32).astype(jnp.bfloat16)


def body(query_rows, key_rows, value_rows, step_sizes, w_gate, w_up, w_down):
    row_count = query_rows.shape[0]
    heads_here = query_rows.shape[1] // HD
    rim_keys, rim_values = passed_along((key_rows, value_rows), "context", 1)
    first_pos = lax.axis_index("context") * row_count
    keys_near = jnp.concatenate([rim_keys, key_rows], axis=0).reshape(
        row_count + WINDOW, heads_here, HD
    )
    values_near = jnp.concatenate([rim_values, value_rows], axis=0).reshape(
        row_count + WINDOW, heads_here, HD
    )
    window_out = window_block(
        query_rows.reshape(row_count, heads_here, HD), keys_near, values_near, first_pos
    )
    window_out = window_out.reshape(row_count, heads_here * HD)
    gathered = (
        lax.all_gather(w_gate, "context", axis=1, tiled=True),
        lax.all_gather(w_up, "context", axis=1, tiled=True),
        lax.all_gather(w_down, "context", axis=1, tiled=True),
    )
    gate_w = gathered[0][0]
    up_w = gathered[1][0]
    down_w = gathered[2][0]
    fast_keys = unit_rows(key_rows.astype(jnp.float32)).astype(jnp.bfloat16)
    fast_queries = unit_rows(query_rows.astype(jnp.float32)).astype(jnp.bfloat16)
    target = (-(step_sizes * value_rows.astype(jnp.float32))).astype(jnp.bfloat16)
    gate_pre = jnp.dot(fast_keys, gate_w, preferred_element_type=jnp.float32)
    up_pre = jnp.dot(fast_keys, up_w, preferred_element_type=jnp.float32)
    sigmoid_gate = jax.nn.sigmoid(gate_pre)
    hidden = (gate_pre * sigmoid_gate * up_pre).astype(jnp.bfloat16)
    back_grad = dot_back(target, down_w)
    d_gate = (back_grad * up_pre * sigmoid_gate * (1.0 + gate_pre * (1.0 - sigmoid_gate))).astype(
        jnp.bfloat16
    )
    d_up = (back_grad * gate_pre * sigmoid_gate).astype(jnp.bfloat16)
    grad_gate = dot_rows(fast_keys, d_gate)
    grad_up = dot_rows(fast_keys, d_up)
    grad_down = dot_rows(hidden, target)
    summed = (
        lax.psum(grad_gate.astype(jnp.bfloat16), "context").astype(jnp.float32),
        lax.psum(grad_up.astype(jnp.bfloat16), "context").astype(jnp.float32),
        lax.psum(grad_down.astype(jnp.bfloat16), "context").astype(jnp.float32),
    )
    updated_gate = renormed(gate_w, summed[0])
    updated_up = renormed(up_w, summed[1])
    updated_down = renormed(down_w, summed[2])
    fast_out = apply_fast(fast_queries, updated_gate, updated_up, updated_down)
    return (window_out, fast_out)


def solution(mesh):
    in_specs = (
        P(("seqs", "context"), "fheads"),
        P(("seqs", "context"), "fheads"),
        P(("seqs", "context"), "fheads"),
        P(("seqs", "context"), "fheads"),
        P("fheads", "context", None),
        P("fheads", "context", None),
        P("fheads", "context", None),
    )
    out_specs = (P(("seqs", "context"), "fheads"), P(("seqs", "context"), "fheads"))
    return jax.shard_map(body, mesh=mesh, in_specs=in_specs, out_specs=out_specs, check_vma=False)
```

profile of v0, /device:TPU:0, one launch (start us, length us, event | category | flops | bytes accessed | tf_op | source)
XLA Modules:
  0.0 101.0 jit_solution(16830201598666049020)
XLA Ops:
  7.2 0.0 copy-start
  7.2 0.0 copy-start.7
  7.2 0.0 all-gather.4.cloned.1.call-start
  7.2 0.7 all-gather.4.cloned.1.call-update
  7.9 0.0 all-gather.8.cloned.1.call-start
  8.0 0.7 all-gather.8.cloned.1.call-update
  8.7 0.0 all-gather.6.cloned.1.call-start
  8.7 0.0 copy-done
  8.7 0.3 copy.14
  9.0 3.3 %collective-permute-start.1 = (bf16[512,768]{0,1:T(8,128)(2,1)S(1)}, bf16[512,768]{0,1:T(8,128)(2,1)}, u32[]{:S(2)}, u32[]{:S(2)}) collective-permute-start(bf16[512,768]{0,1:T(8,128)(2,1)S(1)} %copy.14), channel_id=1, source_target_pairs={{0,16},{1,17},{2,18},{3,19},{4,20},{5,21},{6,22},{7,23},{8,24},{9,... | collective-permute-start | bytes 2359304 | tf_op jit(solution)/shard_map/ppermute | solution.py:14
  12.3 2.2 %collective-permute-start = (bf16[512,768]{1,0:T(8,128)(2,1)S(1)}, bf16[512,768]{1,0:T(8,128)(2,1)}, u32[]{:S(2)}, u32[]{:S(2)}) collective-permute-start(bf16[512,768]{1,0:T(8,128)(2,1)S(1)} %copy-done.7), channel_id=1, source_target_pairs={{0,16},{1,17},{2,18},{3,19},{4,20},{5,21},{6,22},{7,23},{8,24},{9,... | collective-permute-start | bytes 2359304 | tf_op jit(solution)/shard_map/ppermute | solution.py:14
  14.5 0.0 all-gather.6.cloned.1.call-update
  14.5 0.0 all-reduce.3.cloned.1.call-start
  14.5 0.2 fusion.11
  14.8 6.7 %all-gather.4.cloned.1.call-done = bf16[1,768,768]{2,1,0:T(8,128)(2,1)} async-done(((bf16[1,384,768]{2,1,0:T(8,128)(2,1)}), bf16[1,768,768]{2,1,0:T(8,128)(2,1)}) %all-gather.4.cloned.1.call-update) | async-done | bytes 1179664 | tf_op jit(solution)/shard_map/all_gather | solution.py:84
  21.5 3.3 %fusion.21 = f32[512,768]{1,0:T(8,128)} fusion(bf16[1,768,768]{2,1,0:T(8,128)(2,1)} %all-gather.4.cloned.1.call-done, bf16[512,768]{1,0:T(8,128)(2,1)S(1)} %copy-done, f32[512]{0:T(512)S(1)} %add_rsqrt_fusion.3), kind=kOutput, calls=%fused_computation.53 | convolution fusion | flops 605159424 | bytes 3540992 | tf_op jit(solution)/shard_map/dot_general | solution.py:94
  24.8 8.7 %all-gather.8.cloned.1.call-done = bf16[1,768,768]{2,1,0:T(8,128)(2,1)} async-done(((bf16[1,384,768]{2,1,0:T(8,128)(2,1)}), bf16[1,768,768]{2,1,0:T(8,128)(2,1)}) %all-gather.8.cloned.1.call-update) | async-done | bytes 1179664 | tf_op jit(solution)/shard_map/all_gather | solution.py:85
  33.5 2.2 %fusion.16 = f32[512,768]{1,0:T(8,128)S(1)} fusion(bf16[1,768,768]{2,1,0:T(8,128)(2,1)} %all-gather.8.cloned.1.call-done, bf16[512,768]{1,0:T(8,128)(2,1)S(1)} %copy-done, f32[512]{0:T(512)S(1)} %add_rsqrt_fusion.3), kind=kOutput, calls=%fused_computation.48 | convolution fusion | flops 605159424 | bytes 3540992 | tf_op jit(solution)/shard_map/dot_general | solution.py:95
  35.7 1.1 %copy-done.11 = f32[512,768]{1,0:T(8,128)} copy-done((f32[512,768]{1,0:T(8,128)}, f32[512,768]{1,0:T(8,128)S(1)}, u32[]{:S(2)}) %copy-start.11) | copy-done | bytes 1572888
  36.9 0.0 copy-done.9
  36.9 2.1 %convolution_convert_fusion = bf16[768,768]{1,0:T(8,128)(2,1)} fusion(f32[512,768]{1,0:T(8,128)S(1)} %fusion.16, f32[512,768]{1,0:T(8,128)S(1)} %copy-done.9, bf16[512,768]{1,0:T(8,128)(2,1)S(1)} %copy-done.7, f32[512]{0:T(512)S(1)} %bitcast.56), kind=kOutput, calls=%fused_computation.41 | convolution fusion | flops 608501760 | bytes 5113856 | tf_op jit(solution)/shard_map/dot_general | solution.py:42
  39.0 6.5 %all-gather.6.cloned.1.call-done = bf16[1,768,768]{2,1,0:T(8,128)(2,1)} async-done(((bf16[1,384,768]{2,1,0:T(8,128)(2,1)}), bf16[1,768,768]{2,1,0:T(8,128)(2,1)}) %all-gather.6.cloned.1.call-update) | async-done | bytes 1179664 | tf_op jit(solution)/shard_map/all_gather | solution.py:86
  45.5 2.3 %fusion.19 = f32[512,768]{1,0:T(8,128)S(1)} fusion(bf16[1,768,768]{2,1,0:T(8,128)(2,1)} %all-gather.6.cloned.1.call-done, bf16[512,768]{1,0:T(8,128)(2,1)S(1)} %copy-done.7, f32[512]{0:T(512)S(1)} %bitcast.57), kind=kOutput, calls=%fused_computation.51 | convolution fusion | flops 605552640 | bytes 3540992 | tf_op jit(solution)/shard_map/dot_general | solution.py:48
  47.7 0.0 copy-done.10
  47.7 0.0 copy-done.12
  47.7 2.2 %convolution_convert_fusion.2 = bf16[768,768]{1,0:T(8,128)(2,1)} fusion(f32[512,768]{1,0:T(8,128)S(1)} %copy-done.10, f32[512,768]{1,0:T(8,128)S(1)} %fusion.19, f32[512,768]{1,0:T(8,128)S(1)} %copy-done.12, bf16[512,768]{1,0:T(8,128)(2,1)S(1)} %copy-done, f32[512]{0:T(512)S(1)} %add_rsqrt_fusion.3), kind=kOutput, calls=%fused_computation.43 | convolution fusion | flops 609681408 | bytes 6686720 | tf_op jit(solution)/shard_map/dot_general | solution.py:42
  50.0 2.1 %convolution_convert_fusion.1 = bf16[768,768]{1,0:T(8,128)(2,1)} fusion(f32[512,768]{1,0:T(8,128)S(1)} %fusion.19, f32[512,768]{1,0:T(8,128)S(1)} %copy-done.10, bf16[512,768]{1,0:T(8,128)(2,1)S(1)} %copy-done, f32[512]{0:T(512)S(1)} %add_rsqrt_fusion.3), kind=kOutput, calls=%fused_computation.42 | convolution fusion | flops 608108544 | bytes 5113856 | tf_op jit(solution)/shard_map/dot_general | solution.py:42
  52.1 0.0 all-reduce.3.cloned.1.call-update
  52.1 1.1 %copy-done.1 = bf16[512,768]{1,0:T(8,128)(2,1)S(1)} copy-done((bf16[512,768]{1,0:T(8,128)(2,1)S(1)}, bf16[512,768]{1,0:T(8,128)(2,1)}, u32[]{:S(2)}) %copy-start.1) | copy-done | bytes 786456
  53.2 1.2 %copy.16 = bf16[512,768]{0,1:T(8,128)(2,1)} copy(bf16[512,768]{1,0:T(8,128)(2,1)S(1)} %copy-done.1) | data formatting | bytes 1572864 | tf_op args[0]
  54.4 0.2 fusion.9
  54.6 1.8 %compare_and_fusion = pred[512,1024]{0,1:T(8,128)(4,1)} fusion(s32[512]{0:T(512)S(1)} %get-tuple-element.18, s32[512]{0:T(512)S(1)} %get-tuple-element.17, s32[1024]{0:T(1024)S(1)} %iota_add_fusion, pred[1024]{0:T(1024)(128)(4,1)S(1)} %broadcast_compare_fusion), kind=kLoop, calls=%fused_computation.24 | loop fusion | flops 2097152 | bytes 533504 | tf_op jit(solution)/shard_map/and | solution.py:26
  56.4 0.0 collective-permute-done
  56.4 1.5 %pad_maximum_fusion = bf16[1024,768]{1,0:T(8,128)(2,1)S(1)} fusion(bf16[512,768]{1,0:T(8,128)(2,1)} %param.9, bf16[512,768]{1,0:T(8,128)(2,1)} %collective-permute-done), kind=kLoop, calls=%fused_computation.33 | loop fusion | flops 3145728 | bytes 3145728 | tf_op jit(solution)/shard_map/concatenate | solution.py:76
  57.9 1.7 %copy.13 = bf16[1024,768]{0,1:T(8,128)(2,1)} copy(bf16[1024,768]{1,0:T(8,128)(2,1)S(1)} %pad_maximum_fusion) | data formatting | bytes 3145728 | tf_op jit(solution)/shard_map/concatenate | solution.py:76
  59.5 0.0 collective-permute-done.1
  59.5 2.8 %pad_maximum_fusion.1 = bf16[1024,768]{0,1:T(8,128)(2,1)} fusion(bf16[512,768]{0,1:T(8,128)(2,1)S(1)} %copy.14, bf16[512,768]{0,1:T(8,128)(2,1)} %collective-permute-done.1), kind=kLoop, calls=%fused_computation.34 | loop fusion | flops 3145728 | bytes 3145728 | tf_op jit(solution)/shard_map/concatenate | solution.py:73
  62.3 12.6 %fusion.45 = (f32[6,512]{1,0:T(8,128)S(1)}, f32[6,512,1024]{1,2,0:T(8,128)}) fusion(pred[512,1024]{0,1:T(8,128)(4,1)} %compare_and_fusion, bf16[1024,6,128]{0,2,1:T(8,128)(2,1)} %bitcast.53, bf16[512,6,128]{0,2,1:T(8,128)(2,1)} %bitcast.54), kind=kOutput, calls=%fused_computation.81 | convolution fusion | flops 817890304 | bytes 15478784 | tf_op jit(solution)/shard_map/sub | solution.py:35
  74.9 6.0 %fusion.13 = bf16[6,128,512]{2,1,0:T(8,128)(2,1)S(1)} fusion(bf16[1024,6,128]{0,2,1:T(8,128)(2,1)S(1)} %bitcast.52, f32[6,512,1024]{1,2,0:T(8,128)} %get-tuple-element.16, f32[6,512]{1,0:T(8,128)S(1)} %get-tuple-element.15), kind=kOutput, calls=%fused_computation.45 | convolution fusion | flops 811991040 | bytes 14954496 | tf_op jit(solution)/shard_map/hij,jhd->ihd/dot_general | solution.py:37
  80.9 1.2 %copy.20 = bf16[512,768]{1,0:T(8,128)(2,1)} copy(bf16[512,768]{0,1:T(8,128)(2,1)S(1)} %bitcast.55) | data formatting | bytes 1572864
  82.1 3.6 %fusion.6 = (f32[768]{0:T(1024)S(1)}, f32[768]{0:T(1024)S(1)}, f32[768]{0:T(1024)S(1)}, f32[768]{0:T(1024)S(1)}) fusion(bf16[1,768,768]{2,1,0:T(8,128)(2,1)} %all-gather.4.cloned.1.call-done, bf16[768,768]{1,0:T(8,128)(2,1)} %get-tuple-element.13, bf16[768,768]{1,0:T(8,128)(2,1)} %get-tuple-element.14, bf16[1,768,768]{2,1,0:T(8,128)(2,1)} %all-gather.8.cloned.1.call-done), kind=kLoop, calls=%fused_computation.15 | loop fusion | flops 8254464 | bytes 4730880 | tf_op jit(solution)/shard_map/reduce_sum | solution.py:56
  85.7 0.0 copy-start.5
  85.7 0.0 copy-start.6
  85.7 0.6 fusion.8
  86.3 0.6 copy-done.5
  86.9 0.4 copy-done.6
  87.3 2.1 %fusion.14 = f32[512,768]{1,0:T(8,128)} fusion(bf16[768,768]{1,0:T(8,128)(2,1)S(1)} %copy-done.6, bf16[1,768,768]{2,1,0:T(8,128)(2,1)S(1)} %copy-done.5, f32[768]{0:T(1024)S(1)} %add_rsqrt_fusion.2, f32[768]{0:T(1024)S(1)} %multiply_sqrt_fusion.2, bf16[512,768]{1,0:T(8,128)(2,1)S(1)} %copy-done.1, f32[512]{0:T(512)S(1)} %add_rsqrt_fusion.4), kind=kOutput, calls=%fused_computation.46 | convolution fusion | flops 608698368 | bytes 4726784 | tf_op jit(solution)/shard_map/dot_general | solution.py:62
  89.4 5.1 %convolution_convert_fusion.3 = bf16[512,768]{1,0:T(8,128)(2,1)} fusion(bf16[768,768]{1,0:T(8,128)(2,1)} %get-tuple-element.12, bf16[1,768,768]{2,1,0:T(8,128)(2,1)S(1)} %copy-done.3, f32[768]{0:T(1024)S(1)} %get-tuple-element.21, f32[768]{0:T(1024)S(1)} %get-tuple-element.22, f32[512,768]{1,0:T(8,128)} %fusion.14, bf16[768,768]{1,0:T(8,128)(2,1)} %get-tuple-element.14, ...), kind=kOutput, calls=%fused_computation.44 | convolution fusion | flops 1218969600 | bytes 7878656 | tf_op jit(solution)/shard_map/dot_general | solution.py:65
  (25 shorter events, 0.1 us)
Async XLA Ops:
  7.2 1.6 %copy-start = (bf16[512,768]{1,0:T(8,128)(2,1)S(1)}, bf16[512,768]{1,0:T(8,128)(2,1)}, u32[]{:S(2)}) copy-start(bf16[512,768]{1,0:T(8,128)(2,1)} %param.8) | copy-start | bytes 2359300
  7.2 5.1 %copy-start.7 = (bf16[512,768]{1,0:T(8,128)(2,1)S(1)}, bf16[512,768]{1,0:T(8,128)(2,1)}, u32[]{:S(2)}) copy-start(bf16[512,768]{1,0:T(8,128)(2,1)} %param.9) | copy-start | bytes 2359300
  7.2 14.3 %all-gather.4.cloned.1.call-start = ((), (), s32[]{:S(2)}) async-start(), calls=%async_computation | async-start | bytes 1769472 | tf_op jit(solution)/shard_map/all_gather | solution.py:84
  7.9 25.6 %all-gather.8.cloned.1.call-start = ((), (), s32[]{:S(2)}) async-start(), calls=%async_computation.2 | async-start | bytes 1769472 | tf_op jit(solution)/shard_map/all_gather | solution.py:85
  8.7 36.8 %all-gather.6.cloned.1.call-start = ((), (), s32[]{:S(2)}) async-start(), calls=%async_computation.1 | async-start | bytes 1769472 | tf_op jit(solution)/shard_map/all_gather | solution.py:86
  9.0 50.5 %collective-permute-start.1 = (bf16[512,768]{0,1:T(8,128)(2,1)S(1)}, bf16[512,768]{0,1:T(8,128)(2,1)}, u32[]{:S(2)}, u32[]{:S(2)}) collective-permute-start(bf16[512,768]{0,1:T(8,128)(2,1)S(1)} %copy.14), channel_id=1, source_target_pairs={{0,16},{1,17},{2,18},{3,19},{4,20},{5,21},{6,22},{7,23},{8,24},{9,... | collective-permute-start | bytes 2359304 | tf_op jit(solution)/shard_map/ppermute | solution.py:14
  12.3 44.1 %collective-permute-start = (bf16[512,768]{1,0:T(8,128)(2,1)S(1)}, bf16[512,768]{1,0:T(8,128)(2,1)}, u32[]{:S(2)}, u32[]{:S(2)}) collective-permute-start(bf16[512,768]{1,0:T(8,128)(2,1)S(1)} %copy-done.7), channel_id=1, source_target_pairs={{0,16},{1,17},{2,18},{3,19},{4,20},{5,21},{6,22},{7,23},{8,24},{9,... | collective-permute-start | bytes 2359304 | tf_op jit(solution)/shard_map/ppermute | solution.py:14
  14.5 67.6 %all-reduce.3.cloned.1.call-start = ((), (), s32[]{:S(2)}) async-start(), calls=%async_computation.3 | async-start | bytes 7077888 | tf_op jit(solution)/shard_map/psum | solution.py:109
  24.8 12.1 %copy-start.8 = (f32[512,1]{0,1:T(1,128)S(1)}, f32[512,1]{0,1:T(1,128)}, u32[]{:S(2)}) copy-start(f32[512,1]{0,1:T(1,128)} %param.10) | copy-start | bytes 6148
  33.5 3.4 %copy-start.9 = (f32[512,768]{1,0:T(8,128)S(1)}, f32[512,768]{1,0:T(8,128)}, u32[]{:S(2)}) copy-start(f32[512,768]{1,0:T(8,128)} %fusion.21) | copy-start | bytes 4718596
  35.7 1.1 %copy-start.11 = (f32[512,768]{1,0:T(8,128)}, f32[512,768]{1,0:T(8,128)S(1)}, u32[]{:S(2)}) copy-start(f32[512,768]{1,0:T(8,128)S(1)} %fusion.16) | copy-start | bytes 4718596
  45.5 2.3 %copy-start.10 = (f32[512,768]{1,0:T(8,128)S(1)}, f32[512,768]{1,0:T(8,128)}, u32[]{:S(2)}) copy-start(f32[512,768]{1,0:T(8,128)} %fusion.21) | copy-start | bytes 4718596
  45.5 2.3 %copy-start.12 = (f32[512,768]{1,0:T(8,128)S(1)}, f32[512,768]{1,0:T(8,128)}, u32[]{:S(2)}) copy-start(f32[512,768]{1,0:T(8,128)} %copy-done.11) | copy-start | bytes 4718596
  52.1 1.1 %copy-start.1 = (bf16[512,768]{1,0:T(8,128)(2,1)S(1)}, bf16[512,768]{1,0:T(8,128)(2,1)}, u32[]{:S(2)}) copy-start(bf16[512,768]{1,0:T(8,128)(2,1)} %param.7) | copy-start | bytes 2359300
  62.3 12.6 %copy-start.2 = (bf16[1024,768]{0,1:T(8,128)(2,1)S(1)}, bf16[1024,768]{0,1:T(8,128)(2,1)}, u32[]{:S(2)}) copy-start(bf16[1024,768]{0,1:T(8,128)(2,1)} %copy.13) | copy-start | bytes 4718596
  82.1 3.7 %copy-start.3 = (bf16[1,768,768]{2,1,0:T(8,128)(2,1)S(1)}, bf16[1,768,768]{2,1,0:T(8,128)(2,1)}, u32[]{:S(2)}) copy-start(bf16[1,768,768]{2,1,0:T(8,128)(2,1)} %all-gather.6.cloned.1.call-done) | copy-start | bytes 3538948
  82.1 3.7 %copy-start.4 = (bf16[768,768]{1,0:T(8,128)(2,1)S(1)}, bf16[768,768]{1,0:T(8,128)(2,1)}, u32[]{:S(2)}) copy-start(bf16[768,768]{1,0:T(8,128)(2,1)} %get-tuple-element.12) | copy-start | bytes 3538948
  85.7 1.3 %copy-start.5 = (bf16[1,768,768]{2,1,0:T(8,128)(2,1)S(1)}, bf16[1,768,768]{2,1,0:T(8,128)(2,1)}, u32[]{:S(2)}) copy-start(bf16[1,768,768]{2,1,0:T(8,128)(2,1)} %all-gather.4.cloned.1.call-done) | copy-start | bytes 3538948
  85.7 1.6 %copy-start.6 = (bf16[768,768]{1,0:T(8,128)(2,1)S(1)}, bf16[768,768]{1,0:T(8,128)(2,1)}, u32[]{:S(2)}) copy-start(bf16[768,768]{1,0:T(8,128)(2,1)} %get-tuple-element.13) | copy-start | bytes 3538948
Sparse Core Ops, SparseCore 0:
  9.5 11.9 all-gather.3
  23.1 10.3 all-gather.7
  35.0 10.3 all-gather.5
  52.2 25.4 all-reduce.2
where the time goes:
time: 101 us
  matrix products  40 us (40%)
  waiting for transfers between devices  23.3 us (23%)
  between operations  14 us (14%)
  other arithmetic  10.7 us (11%)
  local copies, waits for them, and re-layouts  7.44 us (7%)
  starting transfers between devices  5.59 us (6%)
    sub x1, matrix products, window_block(): powers = jnp.exp(scores - row_max)  12.6 us
    all_gather x1, waiting for transfers between devices, body(): lax.all_gather(w_up, 'context', axis=1, tiled=True)  8.71 us
    all_gather x1, waiting for transfers between devices, body(): lax.all_gather(w_gate, 'context', axis=1, tiled=True)  6.74 us
    all_gather x1, waiting for transfers between devices, body(): lax.all_gather(w_down, 'context', axis=1, tiled=True)  6.47 us
    dot_general x3, matrix products, dot_rows(): lax.dot_general(first_op, second_op, (((0,), (0,)), ((), ())), preferred_...  6.46 us
    dot_general x1, matrix products, window_block(): jnp.einsum('hij,jhd->ihd', weights, values_near, preferred_element_type=j...  6.05 us
    unnamed x29, local copies, waits for them, and re-layouts  5.79 us
    ppermute x2, starting transfers between devices, passed_along(): return lax.ppermute(x, axis, pairs)  5.44 us
  transfers between devices with their start and end apart: 6, of which 3 were waited for; matrix products, arithmetic and copies ran while one was open for 43% of the time, Pallas kernels for 0%

commit v1 on v0

--- a/solution.py
+++ b/solution.py
@@ -6,6 +6,11 @@
 
 HD = 128
 WINDOW = 512
+
+
+def supply_all_runs(my_tile, peer_axis):
+    main = lax.all_gather(my_tile, peer_axis)
+    return jnp.concatenate(main, axis=1)
 
 
 def passed_along(x, axis, by):
@@ -81,7 +86,7 @@
     )
     window_out = window_out.reshape(row_count, heads_here * HD)
     gathered = (
-        lax.all_gather(w_gate, "context", axis=1, tiled=True),
+        supply_all_runs(w_gate, "context"),
         lax.all_gather(w_up, "context", axis=1, tiled=True),
         lax.all_gather(w_down, "context", axis=1, tiled=True),
     )

time: 101 us -> 99.4 us (0.984)
  local copies, waits for them, and re-layouts: 7.44 us -> 5.9 us
    reduce_sum x0 -> x1, other arithmetic: none -> 1.84 us  [renormed(): new_ms = jnp.mean(fresh_rows * fresh_rows, axis=0)]
    unnamed x29 -> x33, local copies, waits for them, and re-layouts: 5.79 us -> 4.24 us
    sub x1, matrix products: 12.6 us -> 11.1 us  [window_block(): powers = jnp.exp(scores - row_max)]
    reduce_sum x2, other arithmetic: 4.14 us -> 2.74 us  [renormed(): old_ms = jnp.mean(initial * initial, axis=0)]
    dot_general x1, matrix products: 6.05 us -> 7.21 us  [window_block(): jnp.einsum('hij,jhd->ihd', weights, values_near, preferred_element_type=j...]
  transfers between devices with their start and end apart: 6 -> 6, of which waited for: 3 -> 3; matrix products, arithmetic and copies ran while one was open for 43% -> 44% of each run, Pallas kernels for 0% -> 0%
where the time goes in v1:
time: 99.4 us; the launch traced here: 99 us
  matrix products  39.7 us (40%)
  waiting for transfers between devices  23 us (23%)
  between operations  14 us (14%)
  other arithmetic  10.7 us (11%)
  local copies, waits for them, and re-layouts  5.9 us (6%)
  starting transfers between devices  5.6 us (6%)
    sub x1, matrix products, window_block(): powers = jnp.exp(scores - row_max)  11.1 us
    all_gather x1, waiting for transfers between devices, body(): lax.all_gather(w_up, 'context', axis=1, tiled=True)  8.71 us
    dot_general x1, matrix products, window_block(): jnp.einsum('hij,jhd->ihd', weights, values_near, preferred_element_type=j...  7.21 us
    dot_general x3, matrix products, dot_rows(): lax.dot_general(first_op, second_op, (((0,), (0,)), ((), ())), preferred_...  6.49 us
    all_gather x1, waiting for transfers between devices, supply_all_runs(): main = lax.all_gather(my_tile, peer_axis)  6.46 us
    all_gather x1, waiting for transfers between devices, body(): lax.all_gather(w_down, 'context', axis=1, tiled=True)  6.44 us
    ppermute x2, starting transfers between devices, passed_along(): return lax.ppermute(x, axis, pairs)  5.44 us
    dot_general x1, matrix products, apply_fast(): jnp.dot(hidden_new, down_w, preferred_element_type=jnp.float32)  5.05 us
  transfers between devices with their start and end apart: 6, of which 3 were waited for; matrix products, arithmetic and copies ran while one was open for 44% of the time, Pallas kernels for 0%

profile of v1, /device:TPU:0, one launch (start us, length us, event | category | flops | bytes accessed | tf_op | source)
XLA Modules:
  0.0 99.0 jit_solution(17460609381326047368)
XLA Ops:
  7.2 0.0 copy-start.1
  7.2 0.0 copy-start.9
  7.2 0.0 all-gather.9.cloned.1.call-start
  7.2 0.7 all-gather.9.cloned.1.call-update
  7.9 0.0 all-gather.7.cloned.1.call-start
  8.0 0.7 all-gather.7.cloned.1.call-update
  8.7 0.0 copy-start.2
  8.7 0.0 all-gather.5.cloned.1.call-start
  8.7 0.3 copy.22
  9.0 3.3 %collective-permute-start.1 = (bf16[512,768]{0,1:T(8,128)(2,1)S(1)}, bf16[512,768]{0,1:T(8,128)(2,1)}, u32[]{:S(2)}, u32[]{:S(2)}) collective-permute-start(bf16[512,768]{0,1:T(8,128)(2,1)S(1)} %copy.22), channel_id=1, source_target_pairs={{0,16},{1,17},{2,18},{3,19},{4,20},{5,21},{6,22},{7,23},{8,24},{9,... | collective-permute-start | bytes 2359304 | tf_op jit(solution)/shard_map/ppermute | solution.py:19
  12.3 2.2 %collective-permute-start = (bf16[512,768]{1,0:T(8,128)(2,1)S(1)}, bf16[512,768]{1,0:T(8,128)(2,1)}, u32[]{:S(2)}, u32[]{:S(2)}) collective-permute-start(bf16[512,768]{1,0:T(8,128)(2,1)S(1)} %copy-done.9), channel_id=1, source_target_pairs={{0,16},{1,17},{2,18},{3,19},{4,20},{5,21},{6,22},{7,23},{8,24},{9,... | collective-permute-start | bytes 2359304 | tf_op jit(solution)/shard_map/ppermute | solution.py:19
  14.5 0.0 all-gather.5.cloned.1.call-update
  14.5 0.0 all-reduce.3.cloned.1.call-start
  14.5 0.2 fusion.10
  14.8 0.2 fusion.8
  15.1 6.5 %all-gather.9.cloned.1.call-done = bf16[2,384,768]{2,1,0:T(8,128)(2,1)} async-done(((bf16[1,384,768]{2,1,0:T(8,128)(2,1)}), bf16[2,384,768]{2,1,0:T(8,128)(2,1)}) %all-gather.9.cloned.1.call-update) | async-done | bytes 1179664 | tf_op jit(solution)/shard_map/all_gather | solution.py:12
  21.5 3.3 %fusion.39 = f32[512,768]{1,0:T(8,128)} fusion(bf16[768,768]{1,0:T(8,128)(2,1)} %bitcast.46, bf16[512,768]{1,0:T(8,128)(2,1)S(1)} %copy-done.1, f32[512]{0:T(512)S(1)} %add_rsqrt_fusion.3), kind=kOutput, calls=%fused_computation.77 | convolution fusion | flops 605159424 | bytes 3540992 | tf_op jit(solution)/shard_map/dot_general | solution.py:99
  24.8 8.7 %all-gather.7.cloned.1.call-done = bf16[1,768,768]{2,1,0:T(8,128)(2,1)} async-done(((bf16[1,384,768]{2,1,0:T(8,128)(2,1)}), bf16[1,768,768]{2,1,0:T(8,128)(2,1)}) %all-gather.7.cloned.1.call-update) | async-done | bytes 1179664 | tf_op jit(solution)/shard_map/all_gather | solution.py:90
  33.5 2.2 %fusion.15 = f32[512,768]{1,0:T(8,128)S(1)} fusion(bf16[1,768,768]{2,1,0:T(8,128)(2,1)} %all-gather.7.cloned.1.call-done, bf16[512,768]{1,0:T(8,128)(2,1)S(1)} %copy-done.1, f32[512]{0:T(512)S(1)} %add_rsqrt_fusion.3), kind=kOutput, calls=%fused_computation.47 | convolution fusion | flops 605159424 | bytes 3540992 | tf_op jit(solution)/shard_map/dot_general | solution.py:100
  35.7 1.1 %copy-done.13 = f32[512,768]{1,0:T(8,128)} copy-done((f32[512,768]{1,0:T(8,128)}, f32[512,768]{1,0:T(8,128)S(1)}, u32[]{:S(2)}) %copy-start.13) | copy-done | bytes 1572888
  36.9 0.0 copy-done.11
  36.9 2.2 %convolution_convert_fusion = bf16[768,768]{1,0:T(8,128)(2,1)} fusion(f32[512,768]{1,0:T(8,128)S(1)} %fusion.15, f32[512,768]{1,0:T(8,128)S(1)} %copy-done.11, bf16[512,768]{1,0:T(8,128)(2,1)S(1)} %copy-done.9, f32[512]{0:T(512)S(1)} %bitcast.52), kind=kOutput, calls=%fused_computation.40 | convolution fusion | flops 608501760 | bytes 5113856 | tf_op jit(solution)/shard_map/dot_general | solution.py:47
  39.0 6.4 %all-gather.5.cloned.1.call-done = bf16[1,768,768]{2,1,0:T(8,128)(2,1)} async-done(((bf16[1,384,768]{2,1,0:T(8,128)(2,1)}), bf16[1,768,768]{2,1,0:T(8,128)(2,1)}) %all-gather.5.cloned.1.call-update) | async-done | bytes 1179664 | tf_op jit(solution)/shard_map/all_gather | solution.py:91
  45.5 2.3 %fusion.18 = f32[512,768]{1,0:T(8,128)S(1)} fusion(bf16[1,768,768]{2,1,0:T(8,128)(2,1)} %all-gather.5.cloned.1.call-done, bf16[512,768]{1,0:T(8,128)(2,1)S(1)} %copy-done.9, f32[512]{0:T(512)S(1)} %bitcast.53), kind=kOutput, calls=%fused_computation.50 | convolution fusion | flops 605552640 | bytes 3540992 | tf_op jit(solution)/shard_map/dot_general | solution.py:53
  47.7 0.0 copy-done.12
  47.7 0.0 copy-done.14
  47.7 2.2 %convolution_convert_fusion.2 = bf16[768,768]{1,0:T(8,128)(2,1)} fusion(f32[512,768]{1,0:T(8,128)S(1)} %copy-done.12, f32[512,768]{1,0:T(8,128)S(1)} %fusion.18, f32[512,768]{1,0:T(8,128)S(1)} %copy-done.14, bf16[512,768]{1,0:T(8,128)(2,1)S(1)} %copy-done.1, f32[512]{0:T(512)S(1)} %add_rsqrt_fusion.3), kind=kOutput, calls=%fused_computation.42 | convolution fusion | flops 609681408 | bytes 6686720 | tf_op jit(solution)/shard_map/dot_general | solution.py:47
  50.0 2.1 %convolution_convert_fusion.1 = bf16[768,768]{1,0:T(8,128)(2,1)} fusion(f32[512,768]{1,0:T(8,128)S(1)} %fusion.18, f32[512,768]{1,0:T(8,128)S(1)} %copy-done.12, bf16[512,768]{1,0:T(8,128)(2,1)S(1)} %copy-done.1, f32[512]{0:T(512)S(1)} %add_rsqrt_fusion.3), kind=kOutput, calls=%fused_computation.41 | convolution fusion | flops 608108544 | bytes 5113856 | tf_op jit(solution)/shard_map/dot_general | solution.py:47
  52.1 0.0 all-reduce.3.cloned.1.call-update
  52.1 1.2 %copy.24 = bf16[512,768]{0,1:T(8,128)(2,1)} copy(bf16[512,768]{1,0:T(8,128)(2,1)S(1)} %copy-done.2) | data formatting | bytes 1572864 | tf_op args[0]
  53.3 1.6 %compare_and_fusion = pred[512,1024]{0,1:T(8,128)(4,1)} fusion(s32[512]{0:T(512)S(1)} %get-tuple-element.18, s32[512]{0:T(512)S(1)} %get-tuple-element.17, s32[1024]{0:T(1024)S(1)} %iota_add_fusion, pred[1024]{0:T(1024)(128)(4,1)S(1)} %broadcast_compare_fusion), kind=kLoop, calls=%fused_computation.23 | loop fusion | flops 2097152 | bytes 533504 | tf_op jit(solution)/shard_map/and | solution.py:31
  54.8 0.0 collective-permute-done
  54.8 1.5 %pad_maximum_fusion = bf16[1024,768]{1,0:T(8,128)(2,1)S(1)} fusion(bf16[512,768]{1,0:T(8,128)(2,1)} %param.9, bf16[512,768]{1,0:T(8,128)(2,1)} %collective-permute-done), kind=kLoop, calls=%fused_computation.32 | loop fusion | flops 3145728 | bytes 3145728 | tf_op jit(solution)/shard_map/concatenate | solution.py:81
  56.3 1.7 %copy.21 = bf16[1024,768]{0,1:T(8,128)(2,1)} copy(bf16[1024,768]{1,0:T(8,128)(2,1)S(1)} %pad_maximum_fusion) | data formatting | bytes 3145728 | tf_op jit(solution)/shard_map/concatenate | solution.py:81
  58.0 0.0 collective-permute-done.1
  58.0 2.6 %pad_maximum_fusion.1 = bf16[1024,768]{0,1:T(8,128)(2,1)} fusion(bf16[512,768]{0,1:T(8,128)(2,1)S(1)} %copy.22, bf16[512,768]{0,1:T(8,128)(2,1)} %collective-permute-done.1), kind=kLoop, calls=%fused_computation.33 | loop fusion | flops 3145728 | bytes 3145728 | tf_op jit(solution)/shard_map/concatenate | solution.py:78
  60.6 11.1 %fusion.42 = (f32[6,512]{1,0:T(8,128)S(1)}, f32[6,512,1024]{1,2,0:T(8,128)}) fusion(pred[512,1024]{0,1:T(8,128)(4,1)} %compare_and_fusion, bf16[1024,6,128]{0,2,1:T(8,128)(2,1)} %bitcast.49, bf16[512,6,128]{0,2,1:T(8,128)(2,1)S(1)} %bitcast.50), kind=kOutput, calls=%fused_computation.78 | convolution fusion | flops 817890304 | bytes 15478784 | tf_op jit(solution)/shard_map/sub | solution.py:40
  71.7 7.2 %fusion.12 = bf16[6,128,512]{2,1,0:T(8,128)(2,1)S(1)} fusion(bf16[1024,6,128]{0,2,1:T(8,128)(2,1)S(1)} %bitcast.48, f32[6,512,1024]{1,2,0:T(8,128)} %get-tuple-element.16, f32[6,512]{1,0:T(8,128)S(1)} %get-tuple-element.15), kind=kOutput, calls=%fused_computation.44 | convolution fusion | flops 811991040 | bytes 14954496 | tf_op jit(solution)/shard_map/hij,jhd->ihd/dot_general | solution.py:42
  78.9 0.0 copy-start
  78.9 1.2 %copy.28 = bf16[512,768]{1,0:T(8,128)(2,1)} copy(bf16[512,768]{0,1:T(8,128)(2,1)S(1)} %bitcast.51) | data formatting | bytes 1572864
  80.1 0.2 copy-done
  80.3 0.3 multiply_reduce_fusion
  80.6 0.0 all-reduce.3.cloned.1.call-done
  80.7 1.8 %multiply_reduce_fusion.3 = f32[768]{0:T(1024)S(1)} fusion(bf16[768,768]{1,0:T(8,128)(2,1)} %get-tuple-element.13, bf16[2,384,768]{2,1,0:T(8,128)(2,1)S(1)} %copy-done), kind=kLoop, calls=%fused_computation.21 | loop fusion | flops 2948352 | bytes 2362368 | tf_op jit(solution)/shard_map/reduce_sum | solution.py:62
  82.6 0.2 copy-done.7
  82.8 2.5 %fusion.6 = (f32[768]{0:T(1024)S(1)}, f32[768]{0:T(1024)S(1)}, f32[768]{0:T(1024)S(1)}, f32[768]{0:T(1024)S(1)}) fusion(bf16[1,768,768]{2,1,0:T(8,128)(2,1)S(1)} %copy-done.5, bf16[768,768]{1,0:T(8,128)(2,1)} %get-tuple-element.14, bf16[768,768]{1,0:T(8,128)(2,1)S(1)} %copy-done.7, bf16[1,768,768]{2,1,0:T(8,128)(2,1)S(1)} %copy-done.6), kind=kLoop, calls=%fused_computation.13 | loop fusion | flops 8254464 | bytes 4730880 | tf_op jit(solution)/shard_map/reduce_sum | solution.py:61
  85.3 2.1 %fusion.13 = f32[512,768]{1,0:T(8,128)} fusion(bf16[768,768]{1,0:T(8,128)(2,1)S(1)} %copy-done.4, bf16[768,768]{1,0:T(8,128)(2,1)S(1)} %bitcast.47, f32[768]{0:T(1024)S(1)} %add_rsqrt_fusion.2, f32[768]{0:T(1024)S(1)} %multiply_sqrt_fusion.2, bf16[512,768]{1,0:T(8,128)(2,1)S(1)} %copy-done.2, f32[512]{0:T(512)S(1)} %add_rsqrt_fusion.4), kind=kOutput, calls=%fused_computation.45 | convolution fusion | flops 608698368 | bytes 4726784 | tf_op jit(solution)/shard_map/dot_general | solution.py:67
  87.4 5.1 %convolution_convert_fusion.3 = bf16[512,768]{1,0:T(8,128)(2,1)} fusion(bf16[768,768]{1,0:T(8,128)(2,1)} %get-tuple-element.12, bf16[1,768,768]{2,1,0:T(8,128)(2,1)} %all-gather.5.cloned.1.call-done, f32[768]{0:T(1024)S(1)} %add_rsqrt_fusion, f32[768]{0:T(1024)S(1)} %multiply_sqrt_fusion, f32[512,768]{1,0:T(8,128)} %fusion.13, ...), kind=kOutput, calls=%fused_computation.43 | convolution fusion | flops 1218969600 | bytes 7878656 | tf_op jit(solution)/shard_map/dot_general | solution.py:70
  (31 shorter events, 0.1 us)
Async XLA Ops:
  7.2 1.6 %copy-start.1 = (bf16[512,768]{1,0:T(8,128)(2,1)S(1)}, bf16[512,768]{1,0:T(8,128)(2,1)}, u32[]{:S(2)}) copy-start(bf16[512,768]{1,0:T(8,128)(2,1)} %param.8) | copy-start | bytes 2359300
  7.2 5.1 %copy-start.9 = (bf16[512,768]{1,0:T(8,128)(2,1)S(1)}, bf16[512,768]{1,0:T(8,128)(2,1)}, u32[]{:S(2)}) copy-start(bf16[512,768]{1,0:T(8,128)(2,1)} %param.9) | copy-start | bytes 2359300
  7.2 14.3 %all-gather.9.cloned.1.call-start = ((), (), s32[]{:S(2)}) async-start(), calls=%async_computation.2 | async-start | bytes 1769472 | tf_op jit(solution)/shard_map/all_gather | solution.py:12
  7.9 25.6 %all-gather.7.cloned.1.call-start = ((), (), s32[]{:S(2)}) async-start(), calls=%async_computation.1 | async-start | bytes 1769472 | tf_op jit(solution)/shard_map/all_gather | solution.py:90
  8.7 6.1 %copy-start.2 = (bf16[512,768]{1,0:T(8,128)(2,1)S(1)}, bf16[512,768]{1,0:T(8,128)(2,1)}, u32[]{:S(2)}) copy-start(bf16[512,768]{1,0:T(8,128)(2,1)} %param.7) | copy-start | bytes 2359300
  8.7 36.8 %all-gather.5.cloned.1.call-start = ((), (), s32[]{:S(2)}) async-start(), calls=%async_computation | async-start | bytes 1769472 | tf_op jit(solution)/shard_map/all_gather | solution.py:91
  9.0 49.0 %collective-permute-start.1 = (bf16[512,768]{0,1:T(8,128)(2,1)S(1)}, bf16[512,768]{0,1:T(8,128)(2,1)}, u32[]{:S(2)}, u32[]{:S(2)}) collective-permute-start(bf16[512,768]{0,1:T(8,128)(2,1)S(1)} %copy.22), channel_id=1, source_target_pairs={{0,16},{1,17},{2,18},{3,19},{4,20},{5,21},{6,22},{7,23},{8,24},{9,... | collective-permute-start | bytes 2359304 | tf_op jit(solution)/shard_map/ppermute | solution.py:19
  12.3 42.5 %collective-permute-start = (bf16[512,768]{1,0:T(8,128)(2,1)S(1)}, bf16[512,768]{1,0:T(8,128)(2,1)}, u32[]{:S(2)}, u32[]{:S(2)}) collective-permute-start(bf16[512,768]{1,0:T(8,128)(2,1)S(1)} %copy-done.9), channel_id=1, source_target_pairs={{0,16},{1,17},{2,18},{3,19},{4,20},{5,21},{6,22},{7,23},{8,24},{9,... | collective-permute-start | bytes 2359304 | tf_op jit(solution)/shard_map/ppermute | solution.py:19
  14.5 66.2 %all-reduce.3.cloned.1.call-start = ((), (), s32[]{:S(2)}) async-start(), calls=%async_computation.3 | async-start | bytes 7077888 | tf_op jit(solution)/shard_map/psum | solution.py:114
  24.8 12.1 %copy-start.10 = (f32[512,1]{0,1:T(1,128)S(1)}, f32[512,1]{0,1:T(1,128)}, u32[]{:S(2)}) copy-start(f32[512,1]{0,1:T(1,128)} %param.10) | copy-start | bytes 6148
  33.5 3.4 %copy-start.11 = (f32[512,768]{1,0:T(8,128)S(1)}, f32[512,768]{1,0:T(8,128)}, u32[]{:S(2)}) copy-start(f32[512,768]{1,0:T(8,128)} %fusion.39) | copy-start | bytes 4718596
  35.7 1.1 %copy-start.13 = (f32[512,768]{1,0:T(8,128)}, f32[512,768]{1,0:T(8,128)S(1)}, u32[]{:S(2)}) copy-start(f32[512,768]{1,0:T(8,128)S(1)} %fusion.15) | copy-start | bytes 4718596
  45.5 2.3 %copy-start.12 = (f32[512,768]{1,0:T(8,128)S(1)}, f32[512,768]{1,0:T(8,128)}, u32[]{:S(2)}) copy-start(f32[512,768]{1,0:T(8,128)} %fusion.39) | copy-start | bytes 4718596
  45.5 2.3 %copy-start.14 = (f32[512,768]{1,0:T(8,128)S(1)}, f32[512,768]{1,0:T(8,128)}, u32[]{:S(2)}) copy-start(f32[512,768]{1,0:T(8,128)} %copy-done.13) | copy-start | bytes 4718596
  58.0 2.6 %copy-start.8 = (bf16[512,768]{0,1:T(8,128)(2,1)S(1)}, bf16[512,768]{0,1:T(8,128)(2,1)}, u32[]{:S(2)}) copy-start(bf16[512,768]{0,1:T(8,128)(2,1)} %copy.24) | copy-start | bytes 2359300
  60.6 11.1 %copy-start.3 = (bf16[1024,768]{0,1:T(8,128)(2,1)S(1)}, bf16[1024,768]{0,1:T(8,128)(2,1)}, u32[]{:S(2)}) copy-start(bf16[1024,768]{0,1:T(8,128)(2,1)} %copy.21) | copy-start | bytes 4718596
  78.9 1.4 %copy-start = (bf16[2,384,768]{2,1,0:T(8,128)(2,1)S(1)}, bf16[2,384,768]{2,1,0:T(8,128)(2,1)}, u32[]{:S(2)}) copy-start(bf16[2,384,768]{2,1,0:T(8,128)(2,1)} %all-gather.9.cloned.1.call-done) | copy-start | bytes 3538948
  80.3 2.2 %copy-start.5 = (bf16[1,768,768]{2,1,0:T(8,128)(2,1)S(1)}, bf16[1,768,768]{2,1,0:T(8,128)(2,1)}, u32[]{:S(2)}) copy-start(bf16[1,768,768]{2,1,0:T(8,128)(2,1)} %all-gather.7.cloned.1.call-done) | copy-start | bytes 3538948
  80.7 1.9 %copy-start.6 = (bf16[1,768,768]{2,1,0:T(8,128)(2,1)S(1)}, bf16[1,768,768]{2,1,0:T(8,128)(2,1)}, u32[]{:S(2)}) copy-start(bf16[1,768,768]{2,1,0:T(8,128)(2,1)} %all-gather.5.cloned.1.call-done) | copy-start | bytes 3538948
  80.7 2.1 %copy-start.7 = (bf16[768,768]{1,0:T(8,128)(2,1)S(1)}, bf16[768,768]{1,0:T(8,128)(2,1)}, u32[]{:S(2)}) copy-start(bf16[768,768]{1,0:T(8,128)(2,1)} %get-tuple-element.12) | copy-start | bytes 3538948
  82.8 2.5 %copy-start.4 = (bf16[768,768]{1,0:T(8,128)(2,1)S(1)}, bf16[768,768]{1,0:T(8,128)(2,1)}, u32[]{:S(2)}) copy-start(bf16[768,768]{1,0:T(8,128)(2,1)} %get-tuple-element.13) | copy-start | bytes 3538948
Sparse Core Ops, SparseCore 0:
  9.5 11.9 all-gather.8
  23.1 10.3 all-gather.6
  35.0 10.3 all-gather.4
  52.2 25.4 all-reduce.2
